TPU v7x, 32 devices: a whole 2x2x4 slice. The times are simulated.
32 devices in a mesh: dp: 8 (over y, x, core), tensor: 4 (over z).
Axes of the slice: x: 2, y: 2, z: 4, core: 2. Of those that a mesh axis runs over, the one named last changes fastest.
Arguments:
- hidden_in: bfloat16 [16, 1024, 768], P('dp', 'tensor'), may hold values from -6 to 6
- cotangent: bfloat16 [16, 1024, 768], P('dp', 'tensor'), may hold values from -6 to 6
- segment_ids: int32 [16, 1024], P('dp'), may hold values from 0 to 6, as said below
- w_qkv: bfloat16 [3, 768, 768], P(None, 'dp', 'tensor'), may hold values from -0.21875 to 0.21875
- w_out: bfloat16 [768, 768], P('tensor', 'dp'), may hold values from -1.25 to 1.25
- w_in: bfloat16 [2, 768, 1152], P(None, 'dp', 'tensor'), may hold values from -0.21875 to 0.21875
- w_down: bfloat16 [1152, 768], P('tensor', 'dp'), may hold values from -0.1875 to 0.1875
- norm_gains: bfloat16 [2, 768], P(None, 'dp'), may hold values from 0.099609375 to 1.8984375
Outputs:
- layer_out: bfloat16 [16, 1024, 768], P('dp', 'tensor')
- grad_input: bfloat16 [16, 1024, 768], P('dp', 'tensor')
- grad_qkv: float32 [3, 768, 768], P(None, 'dp', 'tensor')
- grad_out: float32 [768, 768], P('tensor', 'dp')
- grad_in: float32 [2, 768, 1152], P(None, 'dp', 'tensor')
- grad_down: float32 [1152, 768], P('tensor', 'dp')
- grad_gains: float32 [2, 768], P(None, 'dp')
Inputs may be any that keep to these rules, and one draw needn't show every extreme that they name: `segment_ids`: each row starts with id 0 and its ids never fall, rising by one at each new document; documents are 204 to 2048 tokens long before they are cut at row ends, so only a row's first and last run may be shorter.
All inputs are finite; a program needn't handle non-finite values.
Results may differ from a plain program's by a relative error of at most 0.023.
Values may be sent and summed in bfloat16 or wider, within the bound.
A program may use at most 128 MiB of HBM per device.

v0:
```python
import math

import jax
import jax.numpy as jnp
from jax import lax
from jax.sharding import PartitionSpec as P

HD = 64


EPS = 1e-05
THETA = 160000.0


def layer_norm(value, gain):
    centred = value - jnp.mean(value, axis=-1, keepdims=True)
    variance = jnp.mean(centred * centred, axis=-1, keepdims=True)
    return centred * lax.rsqrt(variance + EPS) * gain


def geglu(gate_up):
    return jax.nn.gelu(gate_up[..., 0, :], approximate=False) * gate_up[..., 1, :]


def positions_of(segments):
    index = lax.broadcasted_iota(jnp.int32, segments.shape, 1)
    change = jnp.concatenate(
        [jnp.ones_like(segments[:, :1]), (segments[:, 1:] != segments[:, :-1]).astype(jnp.int32)],
        axis=1,
    )
    first = lax.cummax(jnp.where(change > 0, index, 0), axis=1)
    return index - first


def rope_tables(positions, head_size):
    half = head_size // 2
    frequency = THETA ** (-2.0 * jnp.arange(half, dtype=jnp.float32) / head_size)
    angle = positions.astype(jnp.float32)[..., None] * frequency
    cosine = jnp.concatenate([jnp.cos(angle), jnp.cos(angle)], axis=-1)[..., None, :]
    sine = jnp.concatenate([jnp.sin(angle), jnp.sin(angle)], axis=-1)[..., None, :]
    return (cosine, sine)


def rotate(value, cosine, sine):
    half = value.shape[-1] // 2
    turned = jnp.concatenate([-value[..., half:], value[..., :half]], axis=-1)
    return value * cosine + turned * sine


def rotate_back(grad, cosine, sine):
    half = grad.shape[-1] // 2
    scaled = grad * sine
    turned = jnp.concatenate([scaled[..., half:], -scaled[..., :half]], axis=-1)
    return grad * cosine + turned


def attend(item):
    query, keys, values, segment = item
    scale = 1.0 / math.sqrt(query.shape[-1])
    scores = jnp.einsum("qhd,khd->hqk", query, keys, preferred_element_type=jnp.float32) * scale
    allowed = (segment[:, None] == segment[None, :])[None]
    scores = jnp.where(allowed, scores, -1e30)
    top = jnp.max(scores, axis=-1, keepdims=True)
    expo = jnp.exp(scores - top)
    total = jnp.sum(expo, axis=-1, keepdims=True)
    probs = expo / total
    mixed = jnp.einsum(
        "hqk,khd->qhd", probs.astype(jnp.bfloat16), values, preferred_element_type=jnp.float32
    )
    return (mixed.astype(jnp.bfloat16), (top + jnp.log(total))[..., 0])


def attend_back(item):
    query, keys, values, segment, logsum, grad_mixed = item
    scale = 1.0 / math.sqrt(query.shape[-1])
    scores = jnp.einsum("qhd,khd->hqk", query, keys, preferred_element_type=jnp.float32) * scale
    allowed = (segment[:, None] == segment[None, :])[None]
    scores = jnp.where(allowed, scores, -1e30)
    probs = jnp.exp(scores - logsum[..., None])
    grad_values = jnp.einsum(
        "hqk,qhd->khd", probs.astype(jnp.bfloat16), grad_mixed, preferred_element_type=jnp.float32
    )
    grad_probs = jnp.einsum("qhd,khd->hqk", grad_mixed, values, preferred_element_type=jnp.float32)
    grad_scores = probs * (grad_probs - jnp.sum(probs * grad_probs, axis=-1, keepdims=True))
    grad_scaled = (grad_scores * scale).astype(jnp.bfloat16)
    grad_query = jnp.einsum("hqk,khd->qhd", grad_scaled, keys, preferred_element_type=jnp.float32)
    grad_keys = jnp.einsum("hqk,qhd->khd", grad_scaled, query, preferred_element_type=jnp.float32)
    return (grad_query, grad_keys, grad_values)


def shards(hidden_in, cotangent, segment_ids, w_qkv, w_out, w_in, w_down, norm_gains):
    batch, local_len = (hidden_in.shape[0], hidden_in.shape[1])
    qkv_all, out_all, in_all, down_all, gains_all = (
        lax.all_gather(w_qkv, "dp", axis=1, tiled=True),
        lax.all_gather(w_out, "dp", axis=1, tiled=True),
        lax.all_gather(w_in, "dp", axis=1, tiled=True),
        lax.all_gather(w_down, "dp", axis=1, tiled=True),
        lax.all_gather(norm_gains, "dp", axis=1, tiled=True),
    )
    gain_one = gains_all[0].astype(jnp.float32)
    gain_two = gains_all[1].astype(jnp.float32)
    hidden_f = hidden_in.astype(jnp.float32)
    normed_one, norm_one_back = jax.vjp(layer_norm, hidden_f, gain_one)
    norm_one_low = normed_one.astype(jnp.bfloat16)
    one_rows = lax.all_gather(norm_one_low, "tensor", axis=1, tiled=True)
    full_len = one_rows.shape[1]
    projected = jnp.einsum("rld,cde->rlce", one_rows, qkv_all, preferred_element_type=jnp.float32)
    local_heads = qkv_all.shape[2] // HD
    cosine, sine = rope_tables(positions_of(segment_ids), HD)
    head_shape = (batch, full_len, local_heads, HD)
    query = rotate(projected[:, :, 0].reshape(head_shape), cosine, sine).astype(jnp.bfloat16)
    keys = rotate(projected[:, :, 1].reshape(head_shape), cosine, sine).astype(jnp.bfloat16)
    values = projected[:, :, 2].reshape(head_shape).astype(jnp.bfloat16)
    mixed_heads, logsum = lax.map(attend, (query, keys, values, segment_ids))
    mixed = mixed_heads.reshape(batch, full_len, local_heads * HD)
    piece = mixed
    attn_local = lax.psum_scatter(
        jnp.einsum("rlk,kd->lrd", piece, out_all, preferred_element_type=jnp.float32).astype(
            jnp.bfloat16
        ),
        "tensor",
        scatter_dimension=0,
        tiled=True,
    ).astype(jnp.float32)
    residual = hidden_f + jnp.transpose(attn_local, (1, 0, 2))
    normed_two, norm_two_back = jax.vjp(layer_norm, residual, gain_two)
    norm_two_low = normed_two.astype(jnp.bfloat16)
    two_rows = lax.all_gather(norm_two_low, "tensor", axis=1, tiled=True)
    gate_up = jnp.einsum("rld,cdf->rlcf", two_rows, in_all, preferred_element_type=jnp.float32)
    product_f, product_back = jax.vjp(geglu, gate_up)
    product = product_f.astype(jnp.bfloat16)
    piece = product
    ffn_local = jnp.transpose(
        lax.psum_scatter(
            jnp.einsum("rlf,fd->lrd", piece, down_all, preferred_element_type=jnp.float32).astype(
                jnp.bfloat16
            ),
            "tensor",
            scatter_dimension=0,
            tiled=True,
        ).astype(jnp.float32),
        (1, 0, 2),
    )
    layer_out = (residual + ffn_local).astype(jnp.bfloat16)
    cot_rows = lax.all_gather(cotangent, "tensor", axis=1, tiled=True)
    grad_down_part = jnp.einsum(
        "rlf,rld->fd", product, cot_rows, preferred_element_type=jnp.float32
    )
    grad_product = jnp.einsum("rld,fd->rlf", cot_rows, down_all, preferred_element_type=jnp.float32)
    grad_gate_up = product_back(grad_product)[0].astype(jnp.bfloat16)
    grad_in_part = jnp.einsum(
        "rld,rlcf->cdf", two_rows, grad_gate_up, preferred_element_type=jnp.float32
    )
    piece = grad_gate_up
    grad_norm_two = jnp.transpose(
        lax.psum_scatter(
            jnp.einsum("rlcf,cdf->lrd", piece, in_all, preferred_element_type=jnp.float32).astype(
                jnp.bfloat16
            ),
            "tensor",
            scatter_dimension=0,
            tiled=True,
        ).astype(jnp.float32),
        (1, 0, 2),
    )
    grad_from_two, gain_two_part = norm_two_back(grad_norm_two)
    grad_residual = cotangent.astype(jnp.float32) + grad_from_two
    residual_rows = lax.all_gather(grad_residual.astype(jnp.bfloat16), "tensor", axis=1, tiled=True)
    grad_out_part = jnp.einsum(
        "rlk,rld->kd", mixed, residual_rows, preferred_element_type=jnp.float32
    )
    grad_mixed = jnp.einsum(
        "rld,kd->rlk", residual_rows, out_all, preferred_element_type=jnp.float32
    )
    grad_mixed = grad_mixed.astype(jnp.bfloat16).reshape(head_shape)
    grad_query, grad_keys, grad_values = lax.map(
        attend_back, (query, keys, values, segment_ids, logsum, grad_mixed)
    )
    grad_query = rotate_back(grad_query, cosine, sine).astype(jnp.bfloat16)
    grad_keys = rotate_back(grad_keys, cosine, sine).astype(jnp.bfloat16)
    grad_raw = jnp.stack([grad_query, grad_keys, grad_values.astype(jnp.bfloat16)], axis=2)
    grad_raw = grad_raw.reshape(batch, full_len, 3, local_heads * HD)
    grad_qkv_part = jnp.einsum(
        "rld,rlce->cde", one_rows, grad_raw, preferred_element_type=jnp.float32
    )
    piece = grad_raw
    grad_norm_one = jnp.transpose(
        lax.psum_scatter(
            jnp.einsum("rlce,cde->lrd", piece, qkv_all, preferred_element_type=jnp.float32).astype(
                jnp.bfloat16
            ),
            "tensor",
            scatter_dimension=0,
            tiled=True,
        ).astype(jnp.float32),
        (1, 0, 2),
    )
    grad_from_one, gain_one_part = norm_one_back(grad_norm_one)
    grad_input = (grad_residual + grad_from_one).astype(jnp.bfloat16)
    gains_part = jnp.stack([gain_one_part, gain_two_part], axis=0)
    grad_qkv, grad_out, grad_in, grad_down, grad_gains = (
        lax.psum_scatter(grad_qkv_part, "dp", scatter_dimension=1, tiled=True),
        lax.psum_scatter(grad_out_part, "dp", scatter_dimension=1, tiled=True),
        lax.psum_scatter(grad_in_part, "dp", scatter_dimension=1, tiled=True),
        lax.psum_scatter(grad_down_part, "dp", scatter_dimension=1, tiled=True),
        lax.psum_scatter(gains_part, "dp", scatter_dimension=1, tiled=True),
    )
    grad_gains = lax.psum(grad_gains, "tensor")
    return (layer_out, grad_input, grad_qkv, grad_out, grad_in, grad_down, grad_gains)


def solution(mesh):
    placed = (
        P("dp", "tensor", None),
        P("dp", "tensor", None),
        P("dp", None),
        P(None, "dp", "tensor"),
        P("tensor", "dp"),
        P(None, "dp", "tensor"),
        P("tensor", "dp"),
        P(None, "dp"),
    )
    return jax.shard_map(
        shards,
        mesh=mesh,
        in_specs=placed,
        out_specs=(
            P("dp", "tensor", None),
            P("dp", "tensor", None),
            P(None, "dp", "tensor"),
            P("tensor", "dp"),
            P(None, "dp", "tensor"),
            P("tensor", "dp"),
            P(None, "dp"),
        ),
        check_vma=False,
    )
```

profile of v0, /device:TPU:0, one launch (start us, length us, event | category | flops | bytes accessed | tf_op | source)
XLA Modules:
  0.0 843.4 jit_solution(16636289737016762979)
XLA Ops:
  10.1 10.4 %all-gather = bf16[8,96,2]{1,2,0:T(2,128)(2,1)S(1)} all-gather(bf16[1,96,2]{1,2,0:T(2,128)(2,1)} %bitcast.407), channel_id=1, replica_groups=mesh['dp'=8,'tensor'=4] {'dp'}, dimensions={0}, use_global_device_ids=true | all-gather | bytes 3456 | tf_op jit(solution)/shard_map/all_gather | solution.py:98
  24.5 13.2 %all_gather.29 = bf16[3,768,192]{2,0,1:T(4,128)(2,1)S(1)} all-gather(bf16[3,96,192]{2,0,1:T(4,128)(2,1)S(1)} %copy.47), channel_id=1, replica_groups=mesh['dp'=8,'tensor'=4] {'dp'}, dimensions={1}, use_global_device_ids=true | all-gather | bytes 995328 | tf_op jit(solution)/shard_map/all_gather | solution.py:94
  40.1 8.9 %all_gather.30 = bf16[192,768]{0,1:T(8,128)(2,1)S(1)} all-gather(bf16[192,96]{0,1:T(8,128)(2,1)S(1)} %copy.49), channel_id=1, replica_groups=mesh['dp'=8,'tensor'=4] {'dp'}, dimensions={1}, use_global_device_ids=true | all-gather | bytes 331776 | tf_op jit(solution)/shard_map/all_gather | solution.py:95
  50.2 36.6 %all-gather.6.cloned.1.call-done = bf16[2,1024,768]{2,1,0:T(8,128)(2,1)} async-done(((bf16[2,256,768]{2,1,0:T(8,128)(2,1)}), bf16[2,1024,768]{2,1,0:T(8,128)(2,1)}) %all-gather.6.cloned.1.call-update) | async-done | bytes 3145744 | tf_op jit(solution)/shard_map/all_gather | solution.py:105
  86.8 4.1 fusion.104
  94.9 29.1 %while.26 = (s32[]{:T(128)}, bf16[2,1024,3,64]{1,3,2,0:T(8,128)(2,1)}, f32[2,3,1024]{2,1,0:T(4,128)S(1)}, bf16[2,1024,3,64]{1,3,2,0:T(8,128)(2,1)}, s32[2,1024]{...) while((s32[]{:T(128)}, ...), condition=%wide.region_7.8_spmd, body=%wide.region_4.7_spmd.sunk | while | flops 844297216 | bytes 47835264 | solution.py:114
  95.6 4.2 fusion.214
  99.9 3.9 fusion.215
  103.8 5.7 fusion.216
  110.2 4.2 fusion.214
  114.4 3.9 fusion.215
  118.3 5.7 fusion.216
  124.0 3.8 convert_bitcast_fusion.1
  128.7 58.4 %reduce-scatter.20.cloned.1.call-done = bf16[256,2,768]{2,0,1:T(8,128)(2,1)} async-done(((bf16[1024,2,768]{2,0,1:T(8,128)(2,1)}), bf16[256,2,768]{2,0,1:T(8,128)(2,1)}) %reduce-scatter.20.cloned.1.call-update) | async-done | bytes 786448 | tf_op jit(solution)/shard_map/reduce_scatter | solution.py:117
  192.2 11.5 %all_gather.32 = bf16[2,768,288]{2,0,1:T(2,128)(2,1)S(1)} all-gather(bf16[2,96,288]{2,0,1:T(2,128)(2,1)S(1)} %copy.51), channel_id=1, replica_groups=mesh['dp'=8,'tensor'=4] {'dp'}, dimensions={1}, use_global_device_ids=true | all-gather | bytes 995328 | tf_op jit(solution)/shard_map/all_gather | solution.py:96
  207.6 9.6 %all_gather.33 = bf16[288,768]{0,1:T(8,128)(2,1)S(1)} all-gather(bf16[288,96]{0,1:T(8,128)(2,1)S(1)} %copy.54), channel_id=1, replica_groups=mesh['dp'=8,'tensor'=4] {'dp'}, dimensions={1}, use_global_device_ids=true | all-gather | bytes 497664 | tf_op jit(solution)/shard_map/all_gather | solution.py:97
  217.3 34.8 %all-gather.10.cloned.1.call-done = bf16[2,1024,768]{2,1,0:T(8,128)(2,1)} async-done(((bf16[2,256,768]{2,1,0:T(8,128)(2,1)}), bf16[2,1024,768]{2,1,0:T(8,128)(2,1)}) %all-gather.10.cloned.1.call-update) | async-done | bytes 3145744 | tf_op jit(solution)/shard_map/all_gather | solution.py:145
  252.1 4.5 fusion.166
  256.6 59.6 %all-gather.8.cloned.1.call-done = bf16[2,1024,768]{2,1,0:T(8,128)(2,1)} async-done(((bf16[2,256,768]{2,1,0:T(8,128)(2,1)}), bf16[2,1024,768]{2,1,0:T(8,128)(2,1)}) %all-gather.8.cloned.1.call-update) | async-done | bytes 3145744 | tf_op jit(solution)/shard_map/all_gather | solution.py:128
  316.2 4.1 fusion.100
  320.3 5.1 multiply_bitcast_fusion
  328.4 4.2 fusion.98
  332.7 59.1 %reduce-scatter.24.cloned.1.call-done = bf16[256,2,768]{2,0,1:T(8,128)(2,1)} async-done(((bf16[1024,2,768]{2,0,1:T(8,128)(2,1)}), bf16[256,2,768]{2,0,1:T(8,128)(2,1)}) %reduce-scatter.24.cloned.1.call-update) | async-done | bytes 786448 | tf_op jit(solution)/shard_map/reduce_scatter | solution.py:156
  399.6 4.8 convolution_bitcast_fusion
  404.5 7.0 fusion.151
  411.5 3.8 copy.85
  418.0 45.0 %all-gather.12.cloned.1.call-done = bf16[2,1024,768]{2,1,0:T(8,128)(2,1)} async-done(((bf16[2,256,768]{2,1,0:T(8,128)(2,1)}), bf16[2,1024,768]{2,1,0:T(8,128)(2,1)}) %all-gather.12.cloned.1.call-update) | async-done | bytes 3145744 | tf_op jit(solution)/shard_map/all_gather | solution.py:168
  463.0 4.0 convolution_convert_fusion
  467.1 108.9 %while.27 = (s32[]{:T(128)}, f32[2,1024,3,64]{1,3,2,0:T(8,128)}, f32[2,1024,3,64]{1,3,2,0:T(8,128)}, bf16[2,1024,3,64]{1,3,2,0:T(8,128)(2,1)}, bf16[2,1024,3,64]...) while((s32[]{:T(128)}, f32[2,1024,3,64]{1,3,2,0:T(8,128)}, ...), condition=%wide.region_17.18_spmd, body=%wide.region_15.17_spmd.sunk | while | flops 2096111616 | bytes 203416752 | solution.py:176
  469.8 4.9 fusion.231
  474.7 6.4 fusion.227
  481.1 19.4 %fusion.230 = f32[2,1024,3,64]{1,3,2,0:T(8,128)} fusion(f32[2,1024,3,64]{1,3,2,0:T(8,128)} %get-tuple-element.340, s32[]{:T(128)S(6)} %copy.123, f32[3,1024,1024]{1,2,0:T(8,128)} %fusion.227, f32[3,1024,1024]{1,2,0:T(8,128)} %copy-done, f32[3,1024]{1,0:T(4,128)S(1)} %dynamic-slice_bitcast_fusion.2, ...), kind=kOutput, calls=%fused_computation.47.clone.1 | convolution fusion | flops 437260288 | bytes 53642240 | tf_op jit(solution)/shard_map/while/body/eval_jaxpr/hqk,qhd->khd/dot_general | solution.py:87
  500.5 21.6 %fusion.229 = f32[2,1024,3,64]{1,3,2,0:T(8,128)} fusion(f32[2,1024,3,64]{1,3,2,0:T(8,128)} %get-tuple-element.339, s32[]{:T(128)S(6)} %copy.123, f32[3,1024,1024]{1,2,0:T(8,128)} %fusion.227, f32[3,1024,1024]{1,2,0:T(8,128)} %copy-done, f32[3,1024]{1,0:T(4,128)S(1)} %dynamic-slice_bitcast_fusion.2, ...), kind=kOutput, calls=%fused_computation.45.clone.1 | convolution fusion | flops 437260288 | bytes 53642240 | tf_op jit(solution)/shard_map/while/body/eval_jaxpr/hqk,khd->qhd/dot_general | solution.py:86
  524.6 4.9 fusion.231
  529.5 6.4 fusion.227
  535.8 19.3 %fusion.230 = f32[2,1024,3,64]{1,3,2,0:T(8,128)} fusion(f32[2,1024,3,64]{1,3,2,0:T(8,128)} %get-tuple-element.340, s32[]{:T(128)S(6)} %copy.123, f32[3,1024,1024]{1,2,0:T(8,128)} %fusion.227, f32[3,1024,1024]{1,2,0:T(8,128)} %copy-done, f32[3,1024]{1,0:T(4,128)S(1)} %dynamic-slice_bitcast_fusion.2, ...), kind=kOutput, calls=%fused_computation.47.clone.1 | convolution fusion | flops 437260288 | bytes 53642240 | tf_op jit(solution)/shard_map/while/body/eval_jaxpr/hqk,qhd->khd/dot_general | solution.py:87
  555.1 20.7 %fusion.229 = f32[2,1024,3,64]{1,3,2,0:T(8,128)} fusion(f32[2,1024,3,64]{1,3,2,0:T(8,128)} %get-tuple-element.339, s32[]{:T(128)S(6)} %copy.123, f32[3,1024,1024]{1,2,0:T(8,128)} %fusion.227, f32[3,1024,1024]{1,2,0:T(8,128)} %copy-done, f32[3,1024]{1,0:T(4,128)S(1)} %dynamic-slice_bitcast_fusion.2, ...), kind=kOutput, calls=%fused_computation.45.clone.1 | convolution fusion | flops 437260288 | bytes 53642240 | tf_op jit(solution)/shard_map/while/body/eval_jaxpr/hqk,khd->qhd/dot_general | solution.py:86
  584.6 3.0 fusion.143
  588.7 4.4 fusion.154
  593.1 3.0 copy.81
  599.0 6.5 fusion.99
  606.9 3.5 convert_bitcast_fusion
  619.6 41.8 %reduce-scatter.28.cloned.1.call-done = f32[96,576]{1,0:T(8,128)} async-done(((f32[768,576]{1,0:T(8,128)}), f32[96,576]{1,0:T(8,128)}) %reduce-scatter.28.cloned.1.call-update) | async-done | bytes 221200
  663.3 60.8 %reduce-scatter.26.cloned.1.call-done = bf16[256,2,768]{2,0,1:T(8,128)(2,1)} async-done(((bf16[1024,2,768]{2,0,1:T(8,128)(2,1)}), bf16[256,2,768]{2,0,1:T(8,128)(2,1)}) %reduce-scatter.26.cloned.1.call-update) | async-done | bytes 786448 | tf_op jit(solution)/shard_map/reduce_scatter | solution.py:188
  729.5 57.1 %reduce-scatter.22.cloned.1.call-done = bf16[256,2,768]{2,0,1:T(8,128)(2,1)} async-done(((bf16[1024,2,768]{2,0,1:T(8,128)(2,1)}), bf16[256,2,768]{2,0,1:T(8,128)(2,1)}) %reduce-scatter.22.cloned.1.call-update) | async-done | bytes 786448 | tf_op jit(solution)/shard_map/reduce_scatter | solution.py:134
  786.6 3.5 add_convert_fusion.1
  790.2 33.3 %reduce-scatter.36.cloned.1.call-done = f32[96,2]{1,0:T(8,128)} async-done(((f32[768,2]{1,0:T(8,128)}), f32[96,2]{1,0:T(8,128)}) %reduce-scatter.36.cloned.1.call-update) | async-done | bytes 784
  824.4 12.2 %psum.7 = f32[2,96]{1,0:T(2,128)} all-reduce(f32[2,96]{1,0:T(2,128)S(1)} %copy.90), channel_id=1, replica_groups=mesh['dp'=8,'tensor'=4] {'tensor'}, use_global_device_ids=true, to_apply=%region_28.29 | all-reduce | flops 192 | bytes 1536 | tf_op jit(solution)/shard_map/psum | solution.py:208
  (231 shorter events, 75.0 us)
Async XLA Ops:
  7.2 15.9 %copy-start.34 = (s32[2,1024]{1,0:T(2,128)S(1)}, s32[2,1024]{1,0:T(2,128)}, u32[]{:S(2)}) copy-start(s32[2,1024]{1,0:T(2,128)} %param.14) | copy-start | bytes 24580
  7.2 17.1 %copy-start.49 = (bf16[192,96]{1,0:T(8,128)(2,1)S(1)}, bf16[192,96]{1,0:T(8,128)(2,1)}, u32[]{:S(2)}) copy-start(bf16[192,96]{1,0:T(8,128)(2,1)} %param.16) | copy-start | bytes 110596
  7.2 17.2 %copy-start.40 = (bf16[3,96,192]{2,1,0:T(8,128)(2,1)S(1)}, bf16[3,96,192]{2,1,0:T(8,128)(2,1)}, u32[]{:S(2)}) copy-start(bf16[3,96,192]{2,1,0:T(8,128)(2,1)} %param.15) | copy-start | bytes 331780
  7.2 79.6 %all-gather.6.cloned.1.call-start = ((), (), s32[]{:S(2)}) async-start(), calls=%async_computation.9 | async-start | bytes 3932160 | tf_op jit(solution)/shard_map/all_gather | solution.py:105
  8.6 15.8 %copy-start.45 = (f32[2,256]{1,0:T(2,128)}, f32[2,256]{1,0:T(2,128)S(1)}, u32[]{:S(2)}) copy-start(f32[2,256]{1,0:T(2,128)S(1)} %broadcast_multiply_fusion.3) | copy-start | bytes 6148
  10.1 10.5 %copy-start.53 = (f32[2,256]{1,0:T(2,128)}, f32[2,256]{1,0:T(2,128)S(1)}, u32[]{:S(2)}) copy-start(f32[2,256]{1,0:T(2,128)S(1)} %fusion.137) | copy-start | bytes 6148
  10.1 14.2 %copy-start.51 = (f32[2,256]{1,0:T(2,128)}, f32[2,256]{1,0:T(2,128)S(1)}, u32[]{:S(2)}) copy-start(f32[2,256]{1,0:T(2,128)S(1)} %fusion.175) | copy-start | bytes 6148
  20.7 375.9 %copy-start.37 = (f32[768]{0:T(1024)}, f32[768]{0:T(1024)S(1)}, u32[]{:S(2)}) copy-start(f32[768]{0:T(1024)S(1)} %get-tuple-element.129) | copy-start | bytes 9220
  23.0 164.1 %reduce-scatter.20.cloned.1.call-start = ((), (), s32[]{:S(2)}) async-start(), calls=%async_computation.10 | async-start | bytes 3932160 | tf_op jit(solution)/shard_map/reduce_scatter | solution.py:117
  37.8 12.4 %copy-start.17 = (bf16[3,768,192]{2,0,1:T(4,128)(2,1)}, bf16[3,768,192]{2,0,1:T(4,128)(2,1)S(1)}, u32[]{:S(2)}) copy-start(bf16[3,768,192]{2,0,1:T(4,128)(2,1)S(1)} %all_gather.29) | copy-start | bytes 2654212
  49.0 75.1 %copy-start.26 = (bf16[192,768]{0,1:T(8,128)(2,1)}, bf16[192,768]{0,1:T(8,128)(2,1)S(1)}, u32[]{:S(2)}) copy-start(bf16[192,768]{0,1:T(8,128)(2,1)S(1)} %all_gather.30) | copy-start | bytes 884740
  50.2 42.6 %copy-start.22 = (f32[2,1024,64]{1,2,0:T(8,128)}, f32[2,1024,64]{1,2,0:T(8,128)S(1)}, u32[]{:S(2)}) copy-start(f32[2,1024,64]{1,2,0:T(8,128)S(1)} %get-tuple-element.191) | copy-start | bytes 1572868
  50.2 42.6 %copy-start.25 = (f32[2,1024,64]{1,2,0:T(8,128)}, f32[2,1024,64]{1,2,0:T(8,128)S(1)}, u32[]{:S(2)}) copy-start(f32[2,1024,64]{1,2,0:T(8,128)S(1)} %get-tuple-element.192) | copy-start | bytes 1572868
  95.6 4.3 copy-start.3
  127.9 59.2 %copy-start.1 = (bf16[2,256,768]{2,1,0:T(8,128)(2,1)S(1)}, bf16[2,256,768]{2,1,0:T(8,128)(2,1)}, u32[]{:S(2)}) copy-start(bf16[2,256,768]{2,1,0:T(8,128)(2,1)} %param.12) | copy-start | bytes 2359300
  127.9 124.2 %all-gather.10.cloned.1.call-start = ((), (), s32[]{:S(2)}) async-start(), calls=%async_computation.13 | async-start | bytes 3932160 | tf_op jit(solution)/shard_map/all_gather | solution.py:145
  128.7 187.5 %all-gather.8.cloned.1.call-start = ((), (), s32[]{:S(2)}) async-start(), calls=%async_computation.11 | async-start | bytes 3932160 | tf_op jit(solution)/shard_map/all_gather | solution.py:128
  188.6 208.0 %copy-start.43 = (f32[2,256]{1,0:T(2,128)}, f32[2,256]{1,0:T(2,128)S(1)}, u32[]{:S(2)}) copy-start(f32[2,256]{1,0:T(2,128)S(1)} %broadcast_multiply_fusion.2) | copy-start | bytes 6148
  190.2 13.5 %copy-start.54 = (f32[2,256]{1,0:T(2,128)}, f32[2,256]{1,0:T(2,128)S(1)}, u32[]{:S(2)}) copy-start(f32[2,256]{1,0:T(2,128)S(1)} %multiply_reduce_fusion.1) | copy-start | bytes 6148
  190.2 13.5 %copy-start.48 = (f32[2,256]{1,0:T(2,128)}, f32[2,256]{1,0:T(2,128)S(1)}, u32[]{:S(2)}) copy-start(f32[2,256]{1,0:T(2,128)S(1)} %fusion.176) | copy-start | bytes 6148
  191.5 200.3 %reduce-scatter.24.cloned.1.call-start = ((), (), s32[]{:S(2)}) async-start(), calls=%async_computation.14 | async-start | bytes 3932160 | tf_op jit(solution)/shard_map/reduce_scatter | solution.py:156
  217.3 39.3 %copy-start.20 = (bf16[288,768]{0,1:T(8,128)(2,1)}, bf16[288,768]{0,1:T(8,128)(2,1)S(1)}, u32[]{:S(2)}) copy-start(bf16[288,768]{0,1:T(8,128)(2,1)S(1)} %all_gather.33) | copy-start | bytes 1327108
  217.3 98.9 %copy-start.30 = (bf16[2,768,288]{1,2,0:T(8,128)(2,1)S(1)}, bf16[2,768,288]{1,2,0:T(8,128)(2,1)}, u32[]{:S(2)}) copy-start(bf16[2,768,288]{1,2,0:T(8,128)(2,1)} %copy.52) | copy-start | bytes 2654212
  327.0 72.6 %copy-start.9 = (bf16[2,1024,288]{1,2,0:T(8,128)(2,1)}, bf16[2,1024,288]{1,2,0:T(8,128)(2,1)S(1)}, u32[]{:S(2)}) copy-start(bf16[2,1024,288]{1,2,0:T(8,128)(2,1)S(1)} %get-tuple-element.170) | copy-start | bytes 3538948
  332.6 64.6 %copy-start.15 = (bf16[2,256,768]{2,1,0:T(8,128)(2,1)S(1)}, bf16[2,256,768]{2,1,0:T(8,128)(2,1)}, u32[]{:S(2)}) copy-start(bf16[2,256,768]{2,1,0:T(8,128)(2,1)} %param.13) | copy-start | bytes 2359300
  332.6 130.4 %all-gather.12.cloned.1.call-start = ((), (), s32[]{:S(2)}) async-start(), calls=%async_computation.15 | async-start | bytes 3932160 | tf_op jit(solution)/shard_map/all_gather | solution.py:168
  399.5 211.3 %reduce-scatter.34.cloned.1.call-start = ((), (), s32[]{:S(2)}) async-start(), calls=%async_computation.20 | async-start | bytes 1327104
  404.4 208.1 %reduce-scatter.32.cloned.1.call-start = ((), (), s32[]{:S(2)}) async-start(), calls=%async_computation.19 | async-start | bytes 2211840
  418.0 49.1 %copy-start.11 = (bf16[2,1024,3,64]{1,3,2,0:T(8,128)(2,1)S(1)}, bf16[2,1024,3,64]{1,3,2,0:T(8,128)(2,1)}, u32[]{:S(2)}) copy-start(bf16[2,1024,3,64]{1,3,2,0:T(8,128)(2,1)} %get-tuple-element.379) | copy-start | bytes 2359300
  418.0 49.1 %copy-start.12 = (bf16[2,1024,3,64]{1,3,2,0:T(8,128)(2,1)S(1)}, bf16[2,1024,3,64]{1,3,2,0:T(8,128)(2,1)}, u32[]{:S(2)}) copy-start(bf16[2,1024,3,64]{1,3,2,0:T(8,128)(2,1)} %get-tuple-element.380) | copy-start | bytes 2359300
  418.0 49.1 %copy-start.13 = (bf16[2,1024,3,64]{1,3,2,0:T(8,128)(2,1)S(1)}, bf16[2,1024,3,64]{1,3,2,0:T(8,128)(2,1)}, u32[]{:S(2)}) copy-start(bf16[2,1024,3,64]{1,3,2,0:T(8,128)(2,1)} %get-tuple-element.381) | copy-start | bytes 2359300
  418.0 49.1 %copy-start.36 = (f32[2,3,1024]{2,1,0:T(4,128)S(1)}, f32[2,3,1024]{2,1,0:T(4,128)}, u32[]{:S(2)}) copy-start(f32[2,3,1024]{2,1,0:T(4,128)} %copy-done.35) | copy-start | bytes 73732
  418.0 199.9 %reduce-scatter.30.cloned.1.call-start = ((), (), s32[]{:S(2)}) async-start(), calls=%async_computation.18 | async-start | bytes 884736
  469.8 4.9 copy-start
  524.6 4.9 copy-start
  584.5 76.9 %reduce-scatter.28.cloned.1.call-start = ((), (), s32[]{:S(2)}) async-start(), calls=%async_computation.17 | async-start | bytes 2211840
  599.0 125.1 %reduce-scatter.26.cloned.1.call-start = ((), (), s32[]{:S(2)}) async-start(), calls=%async_computation.16 | async-start | bytes 3932160 | tf_op jit(solution)/shard_map/reduce_scatter | solution.py:188
  605.5 181.1 %reduce-scatter.22.cloned.1.call-start = ((), (), s32[]{:S(2)}) async-start(), calls=%async_computation.12 | async-start | bytes 3932160 | tf_op jit(solution)/shard_map/reduce_scatter | solution.py:134
  610.4 113.7 %copy-start.2 = (bf16[2,256,768]{2,1,0:T(8,128)(2,1)S(1)}, bf16[2,256,768]{2,1,0:T(8,128)(2,1)}, u32[]{:S(2)}) copy-start(bf16[2,256,768]{2,1,0:T(8,128)(2,1)} %param.12) | copy-start | bytes 2359300
  610.4 113.7 %copy-start.42 = (f32[768]{0:T(1024)S(1)}, f32[768]{0:T(1024)}, u32[]{:S(2)}) copy-start(f32[768]{0:T(1024)} %copy-done.41) | copy-start | bytes 9220
  610.4 113.7 %copy-start.46 = (f32[2,256]{1,0:T(2,128)S(1)}, f32[2,256]{1,0:T(2,128)}, u32[]{:S(2)}) copy-start(f32[2,256]{1,0:T(2,128)} %copy-done.45) | copy-start | bytes 6148
  610.5 213.0 %reduce-scatter.36.cloned.1.call-start = ((), (), s32[]{:S(2)}) async-start(), calls=%async_computation.21 | async-start | bytes 442368
  662.5 124.1 %copy-start.5 = (bf16[256,2,768]{2,0,1:T(8,128)(2,1)S(1)}, bf16[256,2,768]{2,0,1:T(8,128)(2,1)}, u32[]{:S(2)}) copy-start(bf16[256,2,768]{2,0,1:T(8,128)(2,1)} %reduce-scatter.20.cloned.1.call-done) | copy-start | bytes 2359300
  662.5 124.1 %copy-start.8 = (bf16[256,2,768]{2,0,1:T(8,128)(2,1)S(1)}, bf16[256,2,768]{2,0,1:T(8,128)(2,1)}, u32[]{:S(2)}) copy-start(bf16[256,2,768]{2,0,1:T(8,128)(2,1)} %reduce-scatter.24.cloned.1.call-done) | copy-start | bytes 2359300
  662.5 124.1 %copy-start.16 = (bf16[2,256,768]{2,1,0:T(8,128)(2,1)S(1)}, bf16[2,256,768]{2,1,0:T(8,128)(2,1)}, u32[]{:S(2)}) copy-start(bf16[2,256,768]{2,1,0:T(8,128)(2,1)} %param.13) | copy-start | bytes 2359300
  662.5 124.1 %copy-start.38 = (f32[768]{0:T(1024)S(1)}, f32[768]{0:T(1024)}, u32[]{:S(2)}) copy-start(f32[768]{0:T(1024)} %copy-done.37) | copy-start | bytes 9220
  662.5 124.1 %copy-start.44 = (f32[2,256]{1,0:T(2,128)S(1)}, f32[2,256]{1,0:T(2,128)}, u32[]{:S(2)}) copy-start(f32[2,256]{1,0:T(2,128)} %copy-done.43) | copy-start | bytes 6148
  663.3 65.2 %copy-start.56 = (f32[1,768]{1,0:T(1,128)S(1)}, f32[1,768]{1,0:T(1,128)}, u32[]{:S(2)}) copy-start(f32[1,768]{1,0:T(1,128)} %stack.26) | copy-start | bytes 9220
  (26 other events, 65.1 us)
Sparse Core Ops, SparseCore 0:
  23.1 63.6 all-gather.5
  128.0 59.0 reduce-scatter.19
  188.7 63.3 all-gather.9
  254.1 62.0 all-gather.7
  332.7 59.0 reduce-scatter.23
  399.7 63.3 all-gather.11
  466.3 35.3 reduce-scatter.33
  505.1 40.1 reduce-scatter.31
  584.6 33.2 reduce-scatter.29
  621.2 40.1 reduce-scatter.27
  663.7 60.3 reduce-scatter.25
  726.3 60.3 reduce-scatter.21
  789.7 33.8 reduce-scatter.35
where the time goes:
time: 847 us; the launch traced here: 843 us
  waiting for transfers between devices  490 us (58%)
  matrix products  180 us (21%)
  blocking collectives  65.8 us (8%)
  other arithmetic  54.1 us (6%)
  local copies, waits for them, and re-layouts  36 us (4%)
  between operations  14.9 us (2%)
    unnamed x18, waiting for transfers between devices  79 us
    reduce_scatter x1, waiting for transfers between devices, shards(): lax.psum_scatter(jnp.einsum('rlce,cde->lrd', piece, qkv_all, preferred_el...  60.8 us
    all_gather x1, waiting for transfers between devices, shards(): two_rows = lax.all_gather(norm_two_low, 'tensor', axis=1, tiled=True)  59.6 us
    reduce_scatter x1, waiting for transfers between devices, shards(): lax.psum_scatter(jnp.einsum('rlcf,cdf->lrd', piece, in_all, preferred_ele...  59.1 us
    reduce_scatter x1, waiting for transfers between devices, shards(): lax.psum_scatter(jnp.einsum('rlk,kd->lrd', piece, out_all, preferred_elem...  58.4 us
    reduce_scatter x1, waiting for transfers between devices, shards(): lax.psum_scatter(jnp.einsum('rlf,fd->lrd', piece, down_all, preferred_ele...  57.1 us
    all_gather x1, waiting for transfers between devices, shards(): lax.all_gather(grad_residual.astype(jnp.bfloat16), 'tensor', axis=1, tile...  45 us
    dot_general x2, matrix products, attend_back(): jnp.einsum('hqk,khd->qhd', grad_scaled, keys, preferred_element_type=jnp....  42.2 us
  transfers between devices with their start and end apart: 13, of which 11 were waited for; matrix products, arithmetic and copies ran while one was open for 23% of the time, Pallas kernels for 0%

commit v1 on v0

v1 whole, which is shorter than its diff:
```python
import math

import jax
import jax.numpy as jnp
from jax import lax
from jax.sharding import PartitionSpec as P

HD = 64


EPS = 1e-05
THETA = 160000.0


def layer_norm(value, gain):
    centred = value - jnp.mean(value, axis=-1, keepdims=True)
    variance = jnp.mean(centred * centred, axis=-1, keepdims=True)
    return centred * lax.rsqrt(variance + EPS) * gain


def geglu(gate_up):
    return jax.nn.gelu(gate_up[..., 0, :], approximate=False) * gate_up[..., 1, :]


def positions_of(segments):
    index = lax.broadcasted_iota(jnp.int32, segments.shape, 1)
    change = jnp.concatenate(
        [jnp.ones_like(segments[:, :1]), (segments[:, 1:] != segments[:, :-1]).astype(jnp.int32)],
        axis=1,
    )
    first = lax.cummax(jnp.where(change > 0, index, 0), axis=1)
    return index - first


def rope_tables(positions, head_size):
    half = head_size // 2
    frequency = THETA ** (-2.0 * jnp.arange(half, dtype=jnp.float32) / head_size)
    angle = positions.astype(jnp.float32)[..., None] * frequency
    cosine = jnp.concatenate([jnp.cos(angle), jnp.cos(angle)], axis=-1)[..., None, :]
    sine = jnp.concatenate([jnp.sin(angle), jnp.sin(angle)], axis=-1)[..., None, :]
    return (cosine, sine)


def rotate(value, cosine, sine):
    half = value.shape[-1] // 2
    turned = jnp.concatenate([-value[..., half:], value[..., :half]], axis=-1)
    return value * cosine + turned * sine


def rotate_back(grad, cosine, sine):
    half = grad.shape[-1] // 2
    scaled = grad * sine
    turned = jnp.concatenate([scaled[..., half:], -scaled[..., :half]], axis=-1)
    return grad * cosine + turned


def attend(item):
    query, keys, values, allowed = item
    scale = 1.0 / math.sqrt(query.shape[-1])
    scores = jnp.einsum("qhd,khd->hqk", query, keys, preferred_element_type=jnp.float32) * scale
    scores = jnp.where(allowed[None], scores, -1e30)
    top = jnp.max(scores, axis=-1, keepdims=True)
    expo = jnp.exp(scores - top)
    total = jnp.sum(expo, axis=-1, keepdims=True)
    probs = expo / total
    mixed = jnp.einsum(
        "hqk,khd->qhd", probs.astype(jnp.bfloat16), values, preferred_element_type=jnp.float32
    )
    return (mixed.astype(jnp.bfloat16), (top + jnp.log(total))[..., 0])


def attend_back(item):
    query, keys, values, allowed, logsum, grad_mixed = item
    scale = 1.0 / math.sqrt(query.shape[-1])
    scores = jnp.einsum("qhd,khd->hqk", query, keys, preferred_element_type=jnp.float32) * scale
    scores = jnp.where(allowed[None], scores, -1e30)
    probs = jnp.exp(scores - logsum[..., None])
    grad_values = jnp.einsum(
        "hqk,qhd->khd", probs.astype(jnp.bfloat16), grad_mixed, preferred_element_type=jnp.float32
    )
    grad_probs = jnp.einsum("qhd,khd->hqk", grad_mixed, values, preferred_element_type=jnp.float32)
    grad_scores = probs * (grad_probs - jnp.sum(probs * grad_probs, axis=-1, keepdims=True))
    grad_scaled = (grad_scores * scale).astype(jnp.bfloat16)
    grad_query = jnp.einsum("hqk,khd->qhd", grad_scaled, keys, preferred_element_type=jnp.float32)
    grad_keys = jnp.einsum("hqk,qhd->khd", grad_scaled, query, preferred_element_type=jnp.float32)
    return (grad_query, grad_keys, grad_values)


def mm(spec, a, b):
    return jnp.einsum(spec, a, b, preferred_element_type=jnp.float32)


def shards(hidden_in, cotangent, segment_ids, w_qkv, w_out, w_in, w_down, norm_gains):
    ndp, nt = lax.axis_size("dp"), lax.axis_size("tensor")
    bf, f32 = jnp.bfloat16, jnp.float32
    core = lax.axis_index("dp") % 2
    place = lax.axis_index("tensor")
    rows, local_len, width = hidden_in.shape
    half = local_len // 2
    tokens = nt * half

    def swap(v):
        return lax.ppermute(v, "dp", [(i, i ^ 1) for i in range(ndp)])

    def in_order(mine, other, axis):
        return jnp.where(
            core == 0,
            jnp.concatenate([mine, other], axis=axis),
            jnp.concatenate([other, mine], axis=axis),
        )

    def pick(v, index, axis):
        return lax.dynamic_index_in_dim(v, index, axis, keepdims=False)

    def enter(v):
        v = v.reshape(rows, 2, half, width)
        v = in_order(pick(v, core, 1), swap(pick(v, 1 - core, 1)), 0)
        return lax.all_to_all(v, "tensor", 0, 0, tiled=True).reshape(tokens, width)

    def leave(v):
        v = lax.all_to_all(v.reshape(nt, half, width), "tensor", 0, 0, tiled=True)
        v = v.reshape(2, rows, 1, half, width)
        v = in_order(pick(v, core, 0), swap(pick(v, 1 - core, 0)), 1)
        return v.reshape(rows, local_len, width)

    def gather(v):
        return lax.all_gather(lax.all_gather(v, "tensor"), "dp")

    def scatter(v):
        v = lax.psum_scatter(v.astype(bf), "dp", scatter_dimension=0)
        return lax.psum_scatter(v, "tensor", scatter_dimension=0).astype(f32)

    dl, el, fl = w_qkv.shape[1], w_qkv.shape[2], w_in.shape[2]
    ff = fl * nt

    def whole(v, n, cols):
        v = v.reshape(ndp, nt, dl, n, cols)
        return jnp.transpose(v, (3, 0, 2, 1, 4)).reshape(n, ndp * dl, nt * cols)

    def parted(v, n, cols):
        v = v.reshape(n, ndp, dl, nt, cols)
        return jnp.transpose(v, (1, 3, 2, 0, 4)).reshape(ndp, nt, dl, n * cols)

    def flat(v):
        return jnp.transpose(v, (1, 0, 2)).reshape(dl, -1)

    first = gather(jnp.concatenate([flat(w_qkv), w_out.T], axis=1))
    qkv_all = whole(first[..., : 3 * el], 3, el)
    out_t = whole(first[..., 3 * el :], 1, el)[0]
    second = gather(jnp.concatenate([flat(w_in), w_down.T], axis=1))
    in_all = whole(second[..., : 2 * fl], 2, fl)
    down_t = whole(second[..., 2 * fl :], 1, fl)[0]
    gains_all = lax.all_gather(norm_gains, "dp", axis=1, tiled=True)
    gain_one = gains_all[0].astype(f32)
    gain_two = gains_all[1].astype(f32)

    segments = in_order(segment_ids, swap(segment_ids), 0)
    spots = positions_of(segments)
    row_seg = pick(segments, place, 0).reshape(nt, 2, half)
    row_pos = pick(spots, place, 0).reshape(nt, 2, half)
    seg_q = pick(row_seg, core, 1).reshape(tokens)
    seg_k = jnp.concatenate([seg_q, pick(row_seg, 1 - core, 1).reshape(tokens)])
    cosine, sine = rope_tables(pick(row_pos, core, 1).reshape(tokens), HD)
    allowed = seg_q[:, None] == seg_k[None, :]

    hidden_f = enter(hidden_in).astype(f32)
    cot = enter(cotangent)
    normed_one, norm_one_back = jax.vjp(layer_norm, hidden_f, gain_one)
    norm_one_low = normed_one.astype(bf)
    heads = width // HD
    groups = heads // 3
    projected = [mm("ld,de->le", norm_one_low, qkv_all[c]).reshape(tokens, heads, HD) for c in range(3)]
    query = rotate(projected[0], cosine, sine).astype(bf)
    keys = rotate(projected[1], cosine, sine).astype(bf)
    values = projected[2].astype(bf)
    pair = jnp.stack([keys, values])
    pair = jnp.concatenate([pair, swap(pair)], axis=1)

    def grouped(v):
        return jnp.moveaxis(v.reshape(v.shape[0], groups, 3, HD), 1, 0)

    def ungrouped(v):
        return jnp.moveaxis(v, 0, 1).reshape(v.shape[1], width)

    q_g, k_g, v_g = grouped(query), grouped(pair[0]), grouped(pair[1])
    mixed_g, logsum = lax.map(lambda it: attend((*it, allowed)), (q_g, k_g, v_g))
    mixed = ungrouped(mixed_g)
    residual = hidden_f + mm("lk,dk->ld", mixed, out_t)
    normed_two, norm_two_back = jax.vjp(layer_norm, residual, gain_two)
    norm_two_low = normed_two.astype(bf)
    gate_up = jnp.stack([mm("ld,df->lf", norm_two_low, in_all[c]) for c in range(2)], axis=-2)
    product_f, product_back = jax.vjp(geglu, gate_up)
    product = product_f.astype(bf)
    layer_out = leave((residual + mm("lf,df->ld", product, down_t)).astype(bf))

    grad_down_t = mm("ld,lf->df", cot, product)
    grad_gate_up = product_back(mm("ld,df->lf", cot, down_t))[0].astype(bf)
    g_gate, g_up = grad_gate_up[:, 0], grad_gate_up[:, 1]
    grad_in_full = jnp.stack([mm("ld,lf->df", norm_two_low, g).astype(bf) for g in (g_gate, g_up)])
    second_grad = scatter(
        jnp.concatenate([parted(grad_in_full, 2, fl), parted(grad_down_t.astype(bf), 1, fl)], axis=-1)
    )
    grad_norm_two = mm("lf,df->ld", g_gate, in_all[0]) + mm("lf,df->ld", g_up, in_all[1])
    grad_from_two, gain_two_part = norm_two_back(grad_norm_two)
    grad_residual = cot.astype(f32) + grad_from_two
    residual_low = grad_residual.astype(bf)
    grad_out_t = mm("ld,lk->dk", residual_low, mixed).astype(bf)
    grad_mixed = mm("ld,dk->lk", residual_low, out_t).astype(bf).reshape(tokens, heads, HD)
    gq, gk, gv = lax.map(
        lambda it: attend_back((it[0], it[1], it[2], allowed, it[3], it[4])),
        (q_g, k_g, v_g, logsum, grouped(grad_mixed)),
    )
    gq, gk, gv = ungrouped(gq), ungrouped(gk), ungrouped(gv)
    away = swap(jnp.stack([gk[tokens:], gv[tokens:]]).astype(bf)).astype(f32)
    shape = (tokens, heads, HD)
    grad_query = rotate_back(gq.reshape(shape), cosine, sine)
    grad_keys = rotate_back((gk[:tokens] + away[0]).reshape(shape), cosine, sine)
    raws = [
        grad_query.astype(bf).reshape(tokens, width),
        grad_keys.astype(bf).reshape(tokens, width),
        (gv[:tokens] + away[1]).astype(bf),
    ]
    grad_qkv_full = jnp.stack([mm("ld,le->de", norm_one_low, r).astype(bf) for r in raws])
    first_grad = scatter(
        jnp.concatenate([parted(grad_qkv_full, 3, el), parted(grad_out_t, 1, el)], axis=-1)
    )
    grad_norm_one = sum(mm("le,de->ld", raws[c], qkv_all[c]) for c in range(3))
    grad_from_one, gain_one_part = norm_one_back(grad_norm_one)
    grad_input = leave((grad_residual + grad_from_one).astype(bf))
    gains_part = jnp.stack([gain_one_part, gain_two_part], axis=0)
    grad_gains = lax.psum_scatter(gains_part, "dp", scatter_dimension=1, tiled=True)
    grad_gains = lax.psum(grad_gains, "tensor")

    def stacked(v, n, cols):
        return jnp.transpose(v.reshape(dl, n, cols), (1, 0, 2))

    grad_qkv = stacked(first_grad[:, : 3 * el], 3, el)
    grad_out = first_grad[:, 3 * el :].T
    grad_in = stacked(second_grad[:, : 2 * fl], 2, fl)
    grad_down = second_grad[:, 2 * fl :].T
    return (layer_out, grad_input, grad_qkv, grad_out, grad_in, grad_down, grad_gains)


def solution(mesh):
    placed = (
        P("dp", "tensor", None),
        P("dp", "tensor", None),
        P("dp", None),
        P(None, "dp", "tensor"),
        P("tensor", "dp"),
        P(None, "dp", "tensor"),
        P("tensor", "dp"),
        P(None, "dp"),
    )
    return jax.shard_map(
        shards,
        mesh=mesh,
        in_specs=placed,
        out_specs=(
            P("dp", "tensor", None),
            P("dp", "tensor", None),
            P(None, "dp", "tensor"),
            P("tensor", "dp"),
            P(None, "dp", "tensor"),
            P("tensor", "dp"),
            P(None, "dp"),
        ),
        check_vma=False,
    )
```

time: 847 us -> 697 us (0.82); the launches traced: 843 us -> 684 us
  waiting for transfers between devices: 490 us -> 124 us
  local copies, waits for them, and re-layouts: 36 us -> 181 us
  matrix products: 180 us -> 212 us
  other arithmetic: 54.1 us -> 75.1 us
  starting transfers between devices: 1.19 us -> 17.9 us
    all_gather x4 -> x2, waiting for transfers between devices: 176 us -> 0.01 us  [gather(): return lax.all_gather(lax.all_gather(v, 'tensor'), 'dp')]
    reduce_scatter x4, waiting for transfers between devices: 235 us -> 63 us  [the longest x2 34.8 us: scatter(): return lax.psum_scatter(v, 'tensor', scatter_dimension=0).astype(f32)]
    unnamed x18 -> x8, waiting for transfers between devices: 79 us -> 33.4 us
    reshape x0 -> x11, local copies, waits for them, and re-layouts: none -> 40 us  [the longest x2 21.1 us: whole(): v = v.reshape(ndp, nt, dl, n, cols)]
    transpose x0 -> x10, local copies, waits for them, and re-layouts: none -> 34.9 us  [the longest x2 19.7 us: parted(): return jnp.transpose(v, (1, 3, 2, 0, 4)).reshape(ndp, nt, dl, n * cols)]
    another operation x2 -> x7, local copies, waits for them, and re-layouts: 0.58 us -> 30.3 us  [the longest x2 11.6 us: shards(): jnp.stack([mm('ld,lf->df', norm_two_low, g).astype(bf) for g in (g_gate,...]
    slice x3 -> x15, local copies, waits for them, and re-layouts: 1.61 us -> 29.3 us  [the longest x4 9.55 us: shards(): qkv_all[c]]
    all_to_all x0 -> x4, waiting for transfers between devices: none -> 26.5 us  [the longest x2 17.5 us: enter(): return lax.all_to_all(v, 'tensor', 0, 0, tiled=True).reshape(tokens, width)]
  transfers between devices with their start and end apart: 13 -> 18, of which waited for: 11 -> 7; matrix products, arithmetic and copies ran while one was open for 23% -> 50% of each run, Pallas kernels for 0% -> 0%
where the time goes in v1:
time: 697 us; the launch traced here: 684 us
  matrix products  212 us (30%)
  local copies, waits for them, and re-layouts  181 us (26%)
  waiting for transfers between devices  124 us (18%)
  other arithmetic  75.1 us (11%)
  blocking collectives  57.7 us (8%)
  starting transfers between devices  17.9 us (3%)
  between operations  15.6 us (2%)
    dot_general x4, matrix products, attend_back(): jnp.einsum('hqk,qhd->khd', grad_scaled, query, preferred_element_type=jnp...  57.6 us
    dot_general x4, matrix products, attend_back(): jnp.einsum('hqk,khd->qhd', grad_scaled, keys, preferred_element_type=jnp....  55.5 us
    dot_general x21, matrix products, mm(): return jnp.einsum(spec, a, b, preferred_element_type=jnp.float32)  43.8 us
    all_gather x2, blocking collectives, gather(): return lax.all_gather(lax.all_gather(v, 'tensor'), 'dp')  36.5 us
    reduce_scatter x2, waiting for transfers between devices, scatter(): return lax.psum_scatter(v, 'tensor', scatter_dimension=0).astype(f32)  34.8 us
    unnamed x8, waiting for transfers between devices  33.4 us
    reduce_scatter x2, waiting for transfers between devices, scatter(): v = lax.psum_scatter(v.astype(bf), 'dp', scatter_dimension=0)  28.2 us
    reshape x2, local copies, waits for them, and re-layouts, whole(): v = v.reshape(ndp, nt, dl, n, cols)  21.1 us
  transfers between devices with their start and end apart: 18, of which 7 were waited for; matrix products, arithmetic and copies ran while one was open for 50% of the time, Pallas kernels for 0%

profile of v1, /device:TPU:0, one launch (start us, length us, event | category | flops | bytes accessed | tf_op | source)
XLA Modules:
  0.0 684.2 jit_solution(12599172004136583601)
XLA Ops:
  9.4 18.4 %all-gather = bf16[384,768]{1,0:T(8,128)(2,1)} all-gather(bf16[96,768]{1,0:T(8,128)(2,1)S(1)} %copy.59), channel_id=2, replica_groups=mesh['dp'=8,'tensor'=4] {'tensor'}, dimensions={0}, use_global_device_ids=true | all-gather | bytes 737280 | tf_op jit(solution)/shard_map/all_gather | solution.py:127
  28.4 18.1 %all-gather.2 = bf16[384,864]{1,0:T(8,128)(2,1)} all-gather(bf16[96,864]{1,0:T(8,128)(2,1)S(1)} %pad_maximum_fusion.6), channel_id=4, replica_groups=mesh['dp'=8,'tensor'=4] {'tensor'}, dimensions={0}, use_global_device_ids=true | all-gather | bytes 829440 | tf_op jit(solution)/shard_map/all_gather | solution.py:127
  48.1 8.9 %all-gather.4 = bf16[8,96,2]{1,2,0:T(2,128)(2,1)S(1)} all-gather(bf16[1,96,2]{1,2,0:T(2,128)(2,1)S(1)} %bitcast.426), channel_id=1, replica_groups=mesh['dp'=8,'tensor'=4] {'dp'}, dimensions={0}, use_global_device_ids=true | all-gather | bytes 3456 | tf_op jit(solution)/shard_map/all_gather | solution.py:153
  65.3 17.5 %all-to-all-done = bf16[4,128,768]{2,1,0:T(8,128)(2,1)S(1)} async-done(((bf16[4,128,768]{2,1,0:T(8,128)(2,1)}), bf16[4,128,768]{2,1,0:T(8,128)(2,1)S(1)}, u32[]{:S(2)}, u32[]{:S(2)}) %all-to-all-start) | async-done | bytes 786464 | tf_op jit(solution)/shard_map/all_to_all | solution.py:118
  85.2 7.9 %copy.60 = bf16[32,96,768]{1,2,0:T(8,128)(2,1)} copy(bf16[32,96,768]{2,1,0:T(8,128)(2,1)} %all-gather.8.cloned.1.call-done) | data formatting | bytes 9437184 | tf_op jit(solution)/shard_map/all_gather | solution.py:127
  138.4 4.4 slice.183
  147.2 4.6 copy.68
  151.8 4.7 squeeze_reshape.7
  156.4 10.5 %reshape.471 = bf16[8,4,96,2,288]{4,3,2,1,0:T(2,128)(2,1)} reshape(bf16[8,4,96,576]{3,2,1,0:T(8,128)(2,1)} %slice.183) | data formatting | bytes 7077888 | tf_op jit(solution)/shard_map/reshape | solution.py:137
  167.0 10.6 %copy.67 = bf16[8,4,96,2,288]{2,0,4,1,3:T(8,128)(2,1)} copy(bf16[8,4,96,2,288]{4,3,2,1,0:T(2,128)(2,1)} %reshape.471) | data formatting | bytes 7077888 | tf_op jit(solution)/shard_map/reshape | solution.py:137
  177.6 4.9 fusion.139
  182.5 4.7 squeeze.98
  187.2 4.7 squeeze.99
  191.9 4.4 fusion.149
  199.7 29.1 %while.28 = (s32[]{:T(128)}, bf16[4,512,3,64]{1,3,2,0:T(8,128)(2,1)}, f32[4,3,512]{2,1,0:T(4,128)S(1)}, bf16[4,1024,3,64]{1,3,2,0:T(8,128)(2,1)}, bf16[4,512,3,6...) while((s32[]{:T(128)}, ...), condition=%wide.region_7.8_spmd.clone, body=%wide.region_4.7_spmd.clone.sunk | while | flops 422148608 | bytes 22214760 | solution.py:186
  235.0 5.3 multiply_bitcast_fusion
  257.9 5.6 stack.57
  263.5 6.0 stack.58
  269.6 8.1 %maximum_bitcast_fusion.1 = bf16[8,4,96,2,288]{4,1,2,0,3:T(4,128)(2,1)} fusion(bf16[1,8,96,4,288]{4,3,2,1,0:T(4,128)(2,1)} %stack.58, bf16[1,8,96,4,288]{4,3,2,1,0:T(4,128)(2,1)} %stack.57), kind=kLoop, calls=%fused_computation.82 | loop fusion | flops 1769472 | bytes 7077888 | tf_op jit(solution)/shard_map/transpose | solution.py:142
  277.6 9.7 %copy.73 = bf16[8,4,96,2,288]{2,4,3,1,0:T(8,128)(2,1)} copy(bf16[8,4,96,2,288]{4,1,2,0,3:T(4,128)(2,1)} %maximum_bitcast_fusion.1) | data formatting | bytes 7077888 | tf_op jit(solution)/shard_map/transpose | solution.py:142
  291.1 5.6 reshape.484
  296.7 5.4 copy.74
  302.1 7.3 %pad_maximum_fusion = bf16[8,4,96,864]{2,3,1,0:T(8,128)(2,1)} fusion(bf16[8,4,96,288]{2,3,1,0:T(8,128)(2,1)} %bitcast.366, bf16[8,4,96,576]{2,3,1,0:T(8,128)(2,1)} %bitcast.359), kind=kLoop, calls=%fused_computation.79 | loop fusion | flops 10616832 | bytes 10616832 | tf_op jit(solution)/shard_map/concatenate | solution.py:201
  309.5 150.0 %while.29 = (s32[]{:T(128)}, f32[4,512,3,64]{1,3,2,0:T(8,128)}, f32[4,1024,3,64]{1,3,2,0:T(8,128)}, f32[4,1024,3,64]{1,3,2,0:T(8,128)}, bf16[4,1024,3,64]{1,3,2,...) while((s32[]{:T(128)}, f32[4,512,3,64]{1,3,2,0:T(8,128)}, ...), condition=%wide.region_14.15_spmd.clone, body=%wide.region_12.14_spmd.clone.sunk | while | flops 1048056832 | bytes 104660152 | solution.py:209
  314.2 5.1 fusion.223
  319.3 15.2 %fusion.225 = f32[4,512,3,64]{1,3,2,0:T(8,128)} fusion(f32[4,512,3,64]{1,3,2,0:T(8,128)} %get-tuple-element.409, s32[]{:T(128)S(6)} %copy.102, f32[3,512,1024]{2,1,0:T(8,128)} %fusion.223, f32[3,512,1024]{2,1,0:T(8,128)} %copy-done, f32[3,512]{1,0:T(4,128)S(1)} %dynamic-slice_bitcast_fusion.10, pred[512,1024]{1,0:T(8,128)(4,1)S(1)} %broadcast_compare_fusion.5, ...), kind=kOutput, calls=%fused_computation.47.clone.1 | convolution fusion | flops 218630656 | bytes 27018240 | tf_op jit(solution)/shard_map/while/body/eval_jaxpr/hqk,khd->qhd/dot_general | solution.py:84
  334.5 14.7 %fusion.226 = f32[4,1024,3,64]{1,3,2,0:T(8,128)} fusion(f32[4,1024,3,64]{1,3,2,0:T(8,128)} %get-tuple-element.410, s32[]{:T(128)S(6)} %copy.102, f32[3,512,1024]{2,1,0:T(8,128)} %fusion.223, f32[3,512,1024]{2,1,0:T(8,128)} %copy-done, f32[3,512]{1,0:T(4,128)S(1)} %dynamic-slice_bitcast_fusion.10, pred[512,1024]{1,0:T(8,128)(4,1)S(1)} %broadcast_compare_fusion.5, ...), kind=kOutput, calls=%fused_computation.43.clone.1 | convolution fusion | flops 218630656 | bytes 27214848 | tf_op jit(solution)/shard_map/while/body/eval_jaxpr/hqk,qhd->khd/dot_general | solution.py:85
  353.7 4.6 fusion.223
  358.3 13.6 %fusion.225 = f32[4,512,3,64]{1,3,2,0:T(8,128)} fusion(f32[4,512,3,64]{1,3,2,0:T(8,128)} %get-tuple-element.409, s32[]{:T(128)S(6)} %copy.102, f32[3,512,1024]{2,1,0:T(8,128)} %fusion.223, f32[3,512,1024]{2,1,0:T(8,128)} %copy-done, f32[3,512]{1,0:T(4,128)S(1)} %dynamic-slice_bitcast_fusion.10, pred[512,1024]{1,0:T(8,128)(4,1)S(1)} %broadcast_compare_fusion.5, ...), kind=kOutput, calls=%fused_computation.47.clone.1 | convolution fusion | flops 218630656 | bytes 27018240 | tf_op jit(solution)/shard_map/while/body/eval_jaxpr/hqk,khd->qhd/dot_general | solution.py:84
  371.8 14.4 %fusion.226 = f32[4,1024,3,64]{1,3,2,0:T(8,128)} fusion(f32[4,1024,3,64]{1,3,2,0:T(8,128)} %get-tuple-element.410, s32[]{:T(128)S(6)} %copy.102, f32[3,512,1024]{2,1,0:T(8,128)} %fusion.223, f32[3,512,1024]{2,1,0:T(8,128)} %copy-done, f32[3,512]{1,0:T(4,128)S(1)} %dynamic-slice_bitcast_fusion.10, pred[512,1024]{1,0:T(8,128)(4,1)S(1)} %broadcast_compare_fusion.5, ...), kind=kOutput, calls=%fused_computation.43.clone.1 | convolution fusion | flops 218630656 | bytes 27214848 | tf_op jit(solution)/shard_map/while/body/eval_jaxpr/hqk,qhd->khd/dot_general | solution.py:85
  390.7 4.6 fusion.223
  395.2 13.4 %fusion.225 = f32[4,512,3,64]{1,3,2,0:T(8,128)} fusion(f32[4,512,3,64]{1,3,2,0:T(8,128)} %get-tuple-element.409, s32[]{:T(128)S(6)} %copy.102, f32[3,512,1024]{2,1,0:T(8,128)} %fusion.223, f32[3,512,1024]{2,1,0:T(8,128)} %copy-done, f32[3,512]{1,0:T(4,128)S(1)} %dynamic-slice_bitcast_fusion.10, pred[512,1024]{1,0:T(8,128)(4,1)S(1)} %broadcast_compare_fusion.5, ...), kind=kOutput, calls=%fused_computation.47.clone.1 | convolution fusion | flops 218630656 | bytes 27018240 | tf_op jit(solution)/shard_map/while/body/eval_jaxpr/hqk,khd->qhd/dot_general | solution.py:84
  408.6 14.3 %fusion.226 = f32[4,1024,3,64]{1,3,2,0:T(8,128)} fusion(f32[4,1024,3,64]{1,3,2,0:T(8,128)} %get-tuple-element.410, s32[]{:T(128)S(6)} %copy.102, f32[3,512,1024]{2,1,0:T(8,128)} %fusion.223, f32[3,512,1024]{2,1,0:T(8,128)} %copy-done, f32[3,512]{1,0:T(4,128)S(1)} %dynamic-slice_bitcast_fusion.10, pred[512,1024]{1,0:T(8,128)(4,1)S(1)} %broadcast_compare_fusion.5, ...), kind=kOutput, calls=%fused_computation.43.clone.1 | convolution fusion | flops 218630656 | bytes 27214848 | tf_op jit(solution)/shard_map/while/body/eval_jaxpr/hqk,qhd->khd/dot_general | solution.py:85
  427.3 4.6 fusion.223
  431.9 13.4 %fusion.225 = f32[4,512,3,64]{1,3,2,0:T(8,128)} fusion(f32[4,512,3,64]{1,3,2,0:T(8,128)} %get-tuple-element.409, s32[]{:T(128)S(6)} %copy.102, f32[3,512,1024]{2,1,0:T(8,128)} %fusion.223, f32[3,512,1024]{2,1,0:T(8,128)} %copy-done, f32[3,512]{1,0:T(4,128)S(1)} %dynamic-slice_bitcast_fusion.10, pred[512,1024]{1,0:T(8,128)(4,1)S(1)} %broadcast_compare_fusion.5, ...), kind=kOutput, calls=%fused_computation.47.clone.1 | convolution fusion | flops 218630656 | bytes 27018240 | tf_op jit(solution)/shard_map/while/body/eval_jaxpr/hqk,khd->qhd/dot_general | solution.py:84
  445.2 14.3 %fusion.226 = f32[4,1024,3,64]{1,3,2,0:T(8,128)} fusion(f32[4,1024,3,64]{1,3,2,0:T(8,128)} %get-tuple-element.410, s32[]{:T(128)S(6)} %copy.102, f32[3,512,1024]{2,1,0:T(8,128)} %fusion.223, f32[3,512,1024]{2,1,0:T(8,128)} %copy-done, f32[3,512]{1,0:T(4,128)S(1)} %dynamic-slice_bitcast_fusion.10, pred[512,1024]{1,0:T(8,128)(4,1)S(1)} %broadcast_compare_fusion.5, ...), kind=kOutput, calls=%fused_computation.43.clone.1 | convolution fusion | flops 218630656 | bytes 27214848 | tf_op jit(solution)/shard_map/while/body/eval_jaxpr/hqk,qhd->khd/dot_general | solution.py:85
  479.5 4.4 stack.55
  496.0 4.4 stack.53
  500.4 6.5 maximum_bitcast_fusion
  506.9 10.0 %copy.70 = bf16[8,4,96,3,192]{2,4,3,1,0:T(8,128)(2,1)} copy(bf16[8,4,96,3,192]{4,1,2,0,3:T(4,128)(2,1)} %maximum_bitcast_fusion) | data formatting | bytes 7077888 | tf_op jit(solution)/shard_map/transpose | solution.py:142
  516.9 6.7 pad_maximum_fusion.1
  528.9 5.0 all-to-all-start.1
  545.4 9.0 %all-to-all-done.1 = bf16[4,128,768]{2,1,0:T(8,128)(2,1)} async-done(((bf16[4,128,768]{2,1,0:T(8,128)(2,1)}), bf16[4,128,768]{2,1,0:T(8,128)(2,1)}, u32[]{:S(2)}, u32[]{:S(2)}) %all-to-all-start.1) | async-done | bytes 786464 | tf_op jit(solution)/shard_map/all_to_all | solution.py:121
  558.0 28.2 %reduce-scatter.8.cloned.1.call-done = bf16[1,4,96,768]{2,3,1,0:T(8,128)(2,1)} async-done(((bf16[8,4,96,768]{2,3,1,0:T(8,128)(2,1)}), bf16[1,4,96,768]{2,3,1,0:T(8,128)(2,1)}) %reduce-scatter.8.cloned.1.call-update) | async-done | bytes 589840 | tf_op jit(solution)/shard_map/reduce_scatter | solution.py:130
  590.1 32.9 %reduce-scatter.16.cloned.1.call-done = f32[96,2]{1,0:T(8,128)} async-done(((f32[768,2]{1,0:T(8,128)}), f32[96,2]{1,0:T(8,128)}) %reduce-scatter.16.cloned.1.call-update) | async-done | bytes 784
  623.9 12.3 %psum.7 = f32[2,96]{1,0:T(2,128)} all-reduce(f32[2,96]{1,0:T(2,128)S(1)} %copy.77), channel_id=1, replica_groups=mesh['dp'=8,'tensor'=4] {'tensor'}, use_global_device_ids=true, to_apply=%region_24.25 | all-reduce | flops 192 | bytes 1536 | tf_op jit(solution)/shard_map/psum | solution.py:232
  637.1 12.9 %reduce-scatter.14.cloned.1.call-done = bf16[1,96,864]{1,2,0:T(8,128)(2,1)} async-done(((bf16[4,96,864]{1,2,0:T(8,128)(2,1)}), bf16[1,96,864]{1,2,0:T(8,128)(2,1)}) %reduce-scatter.14.cloned.1.call-update) | async-done | bytes 165904 | tf_op jit(solution)/shard_map/reduce_scatter | solution.py:131
  652.5 21.9 %reduce-scatter.10.cloned.1.call-done = bf16[1,96,768]{1,2,0:T(8,128)(2,1)} async-done(((bf16[4,96,768]{1,2,0:T(8,128)(2,1)}), bf16[1,96,768]{1,2,0:T(8,128)(2,1)}) %reduce-scatter.10.cloned.1.call-update) | async-done | bytes 147472 | tf_op jit(solution)/shard_map/reduce_scatter | solution.py:131
  (308 shorter events, 204.5 us)
Async XLA Ops:
  7.2 20.8 %copy-start.44 = (bf16[288,96]{1,0:T(8,128)(2,1)S(1)}, bf16[288,96]{1,0:T(8,128)(2,1)}, u32[]{:S(2)}) copy-start(bf16[288,96]{1,0:T(8,128)(2,1)} %param.18) | copy-start | bytes 165892
  7.2 20.9 %copy-start.41 = (bf16[2,96,288]{2,1,0:T(8,128)(2,1)S(1)}, bf16[2,96,288]{2,1,0:T(8,128)(2,1)}, u32[]{:S(2)}) copy-start(bf16[2,96,288]{2,1,0:T(8,128)(2,1)} %param.17) | copy-start | bytes 331780
  7.2 78.0 %all-gather.8.cloned.1.call-start = ((), (), s32[]{:S(2)}) async-start(), calls=%async_computation.13 | async-start | bytes 5308416 | tf_op jit(solution)/shard_map/all_gather | solution.py:127
  8.3 38.2 %copy-start.48 = (s32[2,1024]{1,0:T(2,128)S(1)}, s32[2,1024]{1,0:T(2,128)}, u32[]{:S(2)}) copy-start(s32[2,1024]{1,0:T(2,128)} %param.14) | copy-start | bytes 24580
  8.4 38.3 %copy-start.37 = (bf16[2,256,768]{2,1,0:T(8,128)(2,1)S(1)}, bf16[2,256,768]{2,1,0:T(8,128)(2,1)}, u32[]{:S(2)}) copy-start(bf16[2,256,768]{2,1,0:T(8,128)(2,1)} %param.12) | copy-start | bytes 2359300
  27.9 19.4 %copy-start.38 = (bf16[2,256,768]{2,1,0:T(8,128)(2,1)S(1)}, bf16[2,256,768]{2,1,0:T(8,128)(2,1)}, u32[]{:S(2)}) copy-start(bf16[2,256,768]{2,1,0:T(8,128)(2,1)} %param.13) | copy-start | bytes 2359300
  27.9 110.6 %all-gather.10.cloned.1.call-start = ((), (), s32[]{:S(2)}) async-start(), calls=%async_computation.14 | async-start | bytes 6193152 | tf_op jit(solution)/shard_map/all_gather | solution.py:127
  28.4 19.7 %copy-start.49 = (bf16[2,96]{1,0:T(2,128)(2,1)S(1)}, bf16[2,96]{1,0:T(2,128)(2,1)}, u32[]{:S(2)}) copy-start(bf16[2,96]{1,0:T(2,128)(2,1)} %param.19) | copy-start | bytes 1156
  46.6 10.7 %collective-permute-start.1 = (s32[2,1024]{1,0:T(2,128)S(1)}, s32[2,1024]{1,0:T(2,128)S(1)}, u32[]{:S(2)}, u32[]{:S(2)}) collective-permute-start(s32[2,1024]{1,0:T(2,128)S(1)} %copy-done.48), channel_id=1, source_target_pairs={{0,4},{4,0},{8,12},{12,8},{16,20},{20,16},{24,28},{28,24},{1,5},{5... | collective-permute-start | bytes 24584 | tf_op jit(solution)/shard_map/ppermute | solution.py:103
  46.7 10.6 %collective-permute-start = (bf16[2,128,768]{2,1,0:T(8,128)(2,1)S(1)}, bf16[2,128,768]{2,1,0:T(8,128)(2,1)S(1)}, u32[]{:S(2)}, u32[]{:S(2)}) collective-permute-start(bf16[2,128,768]{2,1,0:T(8,128)(2,1)S(1)} %get-tuple-element.226), channel_id=1, source_target_pairs={{0,4},{4,0},{8,12},{12,8},{16,20},{20,16},{24,28},{28,24},{1,5},{5... | collective-permute-start | bytes 1179656 | tf_op jit(solution)/shard_map/ppermute | solution.py:103
  48.1 76.6 %collective-permute-start.4 = (bf16[2,128,768]{2,1,0:T(8,128)(2,1)}, bf16[2,128,768]{2,1,0:T(8,128)(2,1)}, u32[]{:S(2)}, u32[]{:S(2)}) collective-permute-start(bf16[2,128,768]{2,1,0:T(8,128)(2,1)} %get-tuple-element.224), channel_id=1, source_target_pairs={{0,4},{4,0},{8,12},{12,8},{16,20},{20,16},{24,28},{28,24},{1,5},{5... | collective-permute-start | bytes 1179656 | tf_op jit(solution)/shard_map/ppermute | solution.py:103
  57.2 26.8 %copy-start.42 = (f32[768]{0:T(1024)}, f32[768]{0:T(1024)S(1)}, u32[]{:S(2)}) copy-start(f32[768]{0:T(1024)S(1)} %get-tuple-element.155) | copy-start | bytes 9220
  58.3 24.4 %all-to-all-start = ((bf16[4,128,768]{2,1,0:T(8,128)(2,1)}), bf16[4,128,768]{2,1,0:T(8,128)(2,1)S(1)}, u32[]{:S(2)}, u32[]{:S(2)}) async-start(bf16[4,128,768]{2,1,0:T(8,128)(2,1)} %maximum_select_fusion), calls=%async_computation | async-start | bytes 1572864 | tf_op jit(solution)/shard_map/all_to_all | solution.py:118
  82.7 146.1 %copy-start.1 = (bf16[4,128,768]{2,1,0:T(8,128)(2,1)}, bf16[4,128,768]{2,1,0:T(8,128)(2,1)S(1)}, u32[]{:S(2)}) copy-start(bf16[4,128,768]{2,1,0:T(8,128)(2,1)S(1)} %all-to-all-done) | copy-start | bytes 2359300
  84.0 9.1 %copy-start.46 = (f32[4,128]{1,0:T(4,128)}, f32[4,128]{1,0:T(4,128)S(1)}, u32[]{:S(2)}) copy-start(f32[4,128]{1,0:T(4,128)S(1)} %fusion.120) | copy-start | bytes 6148
  114.0 3.1 copy-start.28
  117.0 3.2 copy-start.29
  117.0 2.4 copy-start.34
  123.3 3.5 copy-start.15
  124.7 71.6 %collective-permute-start.2 = (bf16[2,512,12,64]{1,3,2,0:T(8,128)(2,1)}, bf16[2,512,12,64]{1,3,2,0:T(8,128)(2,1)}, u32[]{:S(2)}, u32[]{:S(2)}) collective-permute-start(bf16[2,512,12,64]{1,3,2,0:T(8,128)(2,1)} %pad_maximum_fusion.3), channel_id=1, source_target_pairs={{0,4},{4,0},{8,12},{12,8},{16,20},{20,16},{24,28},{28,24},{1,5},{5... | collective-permute-start | bytes 4718600 | tf_op jit(solution)/shard_map/ppermute | solution.py:103
  126.8 65.1 %all-to-all-start.2 = ((bf16[4,128,768]{2,1,0:T(8,128)(2,1)}), bf16[4,128,768]{2,1,0:T(8,128)(2,1)S(1)}, u32[]{:S(2)}, u32[]{:S(2)}) async-start(bf16[4,128,768]{2,1,0:T(8,128)(2,1)} %maximum_select_fusion.2), calls=%async_computation.2 | async-start | bytes 1572864 | tf_op jit(solution)/shard_map/all_to_all | solution.py:118
  130.3 411.6 %reduce-scatter.12.cloned.1.call-start = ((), (), s32[]{:S(2)}) async-start(), calls=%async_computation.11 | async-start | bytes 7962624 | tf_op jit(solution)/shard_map/reduce_scatter | solution.py:130
  191.9 4.4 copy-start.6
  191.9 4.4 copy-start.16
  231.2 19.7 %copy-start.3 = (f32[512,768]{1,0:T(8,128)}, f32[512,768]{1,0:T(8,128)S(1)}, u32[]{:S(2)}) copy-start(f32[512,768]{1,0:T(8,128)S(1)} %get-tuple-element.242) | copy-start | bytes 4718596
  234.9 5.3 copy-start.22
  309.5 276.7 %reduce-scatter.8.cloned.1.call-start = ((), (), s32[]{:S(2)}) async-start(), calls=%async_computation.9 | async-start | bytes 7077888 | tf_op jit(solution)/shard_map/reduce_scatter | solution.py:130
  311.2 3.0 copy-start
  350.7 3.0 copy-start
  387.8 2.9 copy-start
  424.4 2.9 copy-start
  461.0 3.4 copy-start.20
  464.1 9.2 %collective-permute-start.5 = (bf16[2,512,768]{1,2,0:T(8,128)(2,1)}, bf16[2,512,768]{1,2,0:T(8,128)(2,1)}, u32[]{:S(2)}, u32[]{:S(2)}) collective-permute-start(bf16[2,512,768]{1,2,0:T(8,128)(2,1)} %pad_maximum_fusion.4), channel_id=1, source_target_pairs={{0,4},{4,0},{8,12},{12,8},{16,20},{20,16},{24,28},{28,24},{1,5},{5... | collective-permute-start | bytes 4718600 | tf_op jit(solution)/shard_map/ppermute | solution.py:103
  474.9 2.7 copy-start.35
  477.6 6.3 copy-start.27
  487.6 2.8 copy-start.36
  492.7 7.7 %copy-start.10 = (bf16[1,8,96,4,192]{4,3,2,1,0:T(4,128)(2,1)S(1)}, bf16[1,8,96,4,192]{4,3,2,1,0:T(4,128)(2,1)}, u32[]{:S(2)}) copy-start(bf16[1,8,96,4,192]{4,3,2,1,0:T(4,128)(2,1)} %stack.55) | copy-start | bytes 3538948
  506.9 10.0 %copy-start.9 = (bf16[1,8,96,4,192]{2,4,3,1,0:T(8,128)(2,1)S(1)}, bf16[1,8,96,4,192]{2,4,3,1,0:T(8,128)(2,1)}, u32[]{:S(2)}) copy-start(bf16[1,8,96,4,192]{2,4,3,1,0:T(8,128)(2,1)} %copy.71) | copy-start | bytes 3538948
  528.9 25.5 %all-to-all-start.1 = ((bf16[4,128,768]{2,1,0:T(8,128)(2,1)}), bf16[4,128,768]{2,1,0:T(8,128)(2,1)}, u32[]{:S(2)}, u32[]{:S(2)}) async-start(bf16[4,128,768]{2,1,0:T(8,128)(2,1)} %bitcast.403), calls=%async_computation.1 | async-start | bytes 1572864 | tf_op jit(solution)/shard_map/all_to_all | solution.py:121
  533.9 2.8 copy-start.30
  533.9 2.8 copy-start.33
  533.9 89.1 %reduce-scatter.16.cloned.1.call-start = ((), (), s32[]{:S(2)}) async-start(), calls=%async_computation.15 | async-start | bytes 442368
  540.0 2.4 copy-start.8
  541.8 108.1 %reduce-scatter.14.cloned.1.call-start = ((), (), s32[]{:S(2)}) async-start(), calls=%async_computation.12 | async-start | bytes 1105920 | tf_op jit(solution)/shard_map/reduce_scatter | solution.py:131
  554.4 33.0 %all-to-all-start.3 = ((bf16[4,128,768]{2,1,0:T(8,128)(2,1)}), bf16[4,128,768]{2,1,0:T(8,128)(2,1)S(1)}, u32[]{:S(2)}, u32[]{:S(2)}) async-start(bf16[4,128,768]{2,1,0:T(8,128)(2,1)} %bitcast.379), calls=%async_computation.3 | async-start | bytes 1572864 | tf_op jit(solution)/shard_map/all_to_all | solution.py:121
  557.9 116.5 %reduce-scatter.10.cloned.1.call-start = ((), (), s32[]{:S(2)}) async-start(), calls=%async_computation.10 | async-start | bytes 983040 | tf_op jit(solution)/shard_map/reduce_scatter | solution.py:131
  587.4 1.8 collective-permute-start.3
  587.5 48.6 %collective-permute-start.6 = (bf16[2,1,128,768]{3,2,1,0:T(8,128)(2,1)S(1)}, bf16[2,1,128,768]{3,2,1,0:T(8,128)(2,1)S(1)}, u32[]{:S(2)}, u32[]{:S(2)}) collective-permute-start(bf16[2,1,128,768]{3,2,1,0:T(8,128)(2,1)S(1)} %get-tuple-element.220), channel_id=1, source_target_pairs={{0,4},{4,0},{8,12},{12,8},{16,20},{20,16},{24,28},{28,24},{1,5},{5... | collective-permute-start | bytes 1179656 | tf_op jit(solution)/shard_map/ppermute | solution.py:103
  (27 other events, 38.5 us)
Sparse Core Ops, SparseCore 0:
  28.0 40.4 all-gather.7
  70.4 42.0 all-gather.9
  309.6 65.9 reduce-scatter.11
  523.8 62.3 reduce-scatter.7
  589.1 33.8 reduce-scatter.15
  625.2 24.7 reduce-scatter.13
  652.2 22.1 reduce-scatter.9
